TPU v7x, 32 devices: a whole 2x2x4 slice. The times are simulated.
32 devices in a mesh: seq: 8 (over y, x, core), clip: 4 (over z).
Axes of the slice: x: 2, y: 2, z: 4, core: 2. Of those that a mesh axis runs over, the one named last changes fastest.
Arguments:
- queries: bfloat16 [4, 4096, 512], P('clip', 'seq'), may hold values from -8 to 8
- keys: bfloat16 [4, 4096, 512], P('clip', 'seq'), may hold values from -8 to 8
- values: bfloat16 [4, 4096, 512], P('clip', 'seq'), may hold values from -6 to 6
- out_cotangent: bfloat16 [4, 4096, 1024], P('clip', 'seq'), may hold values from -6 to 6
- visible_counts: int32 [4, 8], P('clip'), may hold values from 1 to 96, 384 in all within a row
- span_offset: int32 [4, 8], P('clip'), may hold values from 0 to 511
- out_weight: bfloat16 [512, 1024], P('seq'), may hold values from -0.1875 to 0.1875
Outputs:
- query_grads: bfloat16 [4, 4096, 512], P('clip', 'seq')
- key_grads: bfloat16 [4, 4096, 512], P('clip', 'seq')
- value_grads: bfloat16 [4, 4096, 512], P('clip', 'seq')
- weight_grad: float32 [512, 1024], P('seq')
Inputs may be any that keep to these rules, and one draw needn't show every extreme that they name: `visible_counts`: in each clip the 8 counts sum to 384, and the largest is exactly 96.
All inputs are finite; a program needn't handle non-finite values.
Results may differ from a plain program's by a relative error of at most 0.014.
Values may be sent and summed in bfloat16 or wider, within the bound.
No kernel may reach another device: no remote copies, remote signals or barrier semaphores. Data moves between devices by JAX's collectives and lax.ppermute only.
A program may use at most 64 MiB of HBM per device.

v0:
```python
import jax
import jax.numpy as jnp
from jax import lax
from jax.sharding import PartitionSpec as P

HEADS = 8
HD = 64
VIS_DEV = 48
MAXV = 96


def pick_entry(table, position):
    order = jnp.arange(table.shape[0], dtype=jnp.int32)
    chosen = jnp.where(order[None, :] == position[:, None], table[None, :], 0)
    return jnp.sum(chosen, axis=1)


def split_heads(block):
    return block.reshape(block.shape[0], HEADS, HD).transpose(1, 0, 2)


def join_heads(block):
    return block.transpose(1, 0, 2).reshape(block.shape[1], HEADS * HD)


def query_side(parts):
    query_head, key_head, value_head, dout_head = parts
    factor = HD ** (-0.5)
    scores = (
        lax.dot_general(
            query_head, key_head, (((1,), (1,)), ((), ())), preferred_element_type=jnp.float32
        )
        * factor
    )
    peak_score = jnp.max(scores, axis=1, keepdims=True)
    log_total = peak_score + jnp.log(jnp.sum(jnp.exp(scores - peak_score), axis=1, keepdims=True))
    weights = jnp.exp(scores - log_total)
    weights_low = weights.astype(jnp.bfloat16)
    attended = jnp.dot(weights_low, value_head, preferred_element_type=jnp.float32).astype(
        jnp.bfloat16
    )
    inner_sum = jnp.sum(
        dout_head.astype(jnp.float32) * attended.astype(jnp.float32), axis=1, keepdims=True
    )
    dweights = lax.dot_general(
        dout_head, value_head, (((1,), (1,)), ((), ())), preferred_element_type=jnp.float32
    )
    dscores = (weights * (dweights - inner_sum)).astype(jnp.bfloat16)
    grad_query = (jnp.dot(dscores, key_head, preferred_element_type=jnp.float32) * factor).astype(
        jnp.bfloat16
    )
    return (attended, grad_query, log_total[:, 0], inner_sum[:, 0])


def key_side_add(query_piece, dout_piece, log_piece, inner_piece, key_heads, value_heads):
    factor = HD ** (-0.5)

    def one_head(parts):
        query_head, dout_head, log_head, inner_head, key_head, value_head = parts
        scores = (
            lax.dot_general(
                query_head, key_head, (((1,), (1,)), ((), ())), preferred_element_type=jnp.float32
            )
            * factor
        )
        weights = jnp.exp(scores - log_head[:, None])
        weights_low = weights.astype(jnp.bfloat16)
        value_part = lax.dot_general(
            weights_low, dout_head, (((0,), (0,)), ((), ())), preferred_element_type=jnp.float32
        )
        dweights = lax.dot_general(
            dout_head, value_head, (((1,), (1,)), ((), ())), preferred_element_type=jnp.float32
        )
        dscores = (weights * (dweights - inner_head[:, None])).astype(jnp.bfloat16)
        key_part = lax.dot_general(
            dscores, query_head, (((0,), (0,)), ((), ())), preferred_element_type=jnp.float32
        )
        return (key_part, value_part)

    key_parts, value_parts = lax.map(
        one_head,
        (
            split_heads(query_piece),
            split_heads(dout_piece),
            log_piece.T,
            inner_piece.T,
            key_heads,
            value_heads,
        ),
    )
    return (key_parts, value_parts)


def local(queries, keys, values, out_cotangent, visible_counts, span_offset, out_weight):
    devices = lax.axis_size("seq")
    device = lax.axis_index("seq")
    frames = queries.shape[1]
    visible_rows = VIS_DEV
    capacity = MAXV // devices
    counts = visible_counts[0]
    offsets = span_offset[0]
    shard_ends = jnp.cumsum(counts)
    starts = shard_ends - counts
    this_device = device.reshape(1)
    count_here = pick_entry(counts, this_device)[0]
    start_here = pick_entry(starts, this_device)[0]
    span_begin = pick_entry(offsets, this_device)[0] % (count_here + 1)
    masked = frames - count_here
    send_slots = jnp.arange(devices * capacity, dtype=jnp.int32)
    peer_index = send_slots // capacity
    within = send_slots % capacity
    first_slot = (start_here - peer_index + devices - 1) // devices
    global_index = (first_slot + within) * devices + peer_index
    ranked = global_index - start_here
    live_slot = ranked < count_here
    frame_of = jnp.clip(jnp.where(ranked < span_begin, ranked, ranked + masked), 0, frames - 1)

    def outgoing(block):
        return jnp.where(
            live_slot[:, None], jnp.take(block[0], frame_of, axis=0), jnp.zeros((), block.dtype)
        )

    arrived = (
        lax.all_to_all(outgoing(queries), "seq", split_axis=0, concat_axis=0, tiled=True),
        lax.all_to_all(outgoing(keys), "seq", split_axis=0, concat_axis=0, tiled=True),
        lax.all_to_all(outgoing(values), "seq", split_axis=0, concat_axis=0, tiled=True),
        lax.all_to_all(outgoing(out_cotangent), "seq", split_axis=0, concat_axis=0, tiled=True),
    )
    packed_slot = jnp.arange(visible_rows, dtype=jnp.int32)
    packed_index = packed_slot * devices + device
    owner_shard = jnp.sum((shard_ends[None, :] <= packed_index[:, None]).astype(jnp.int32), axis=1)
    owner_first = (pick_entry(starts, owner_shard) - device + devices - 1) // devices
    arrived_row = owner_shard * capacity + packed_slot - owner_first
    query_pack = jnp.take(arrived[0], arrived_row, axis=0)
    key_pack = jnp.take(arrived[1], arrived_row, axis=0)
    value_pack = jnp.take(arrived[2], arrived_row, axis=0)
    cotangent_pack = jnp.take(arrived[3], arrived_row, axis=0)
    output_grad = lax.dot_general(
        cotangent_pack,
        lax.all_gather(out_weight, "seq", axis=0, tiled=True),
        (((1,), (1,)), ((), ())),
        preferred_element_type=jnp.float32,
    ).astype(jnp.bfloat16)
    key_all, value_all = (
        lax.all_gather(key_pack, "seq", axis=0, tiled=True),
        lax.all_gather(value_pack, "seq", axis=0, tiled=True),
    )
    attended, query_grad, log_totals, inner_sums = lax.map(
        query_side,
        (
            split_heads(query_pack),
            split_heads(key_all),
            split_heads(value_all),
            split_heads(output_grad),
        ),
    )
    attended = join_heads(attended)
    query_grad = join_heads(query_grad)
    log_rows = log_totals.T
    inner_rows = inner_sums.T
    partial_term = lax.dot_general(
        attended, cotangent_pack, (((0,), (0,)), ((), ())), preferred_element_type=jnp.float32
    )
    seq_sum = lax.psum_scatter(
        partial_term.astype(jnp.bfloat16), "seq", scatter_dimension=0, tiled=True
    )
    clip_sum = lax.psum(seq_sum, "clip").astype(jnp.float32)
    weight_grad = clip_sum * (lax.axis_size("clip") * visible_rows * devices) ** (-0.5)
    log_every, inner_every = (
        lax.all_gather(log_rows, "seq", axis=0, tiled=True),
        lax.all_gather(inner_rows, "seq", axis=0, tiled=True),
    )
    key_heads = split_heads(key_pack)
    value_heads = split_heads(value_pack)
    key_sum, value_sum = key_side_add(
        lax.all_gather(query_pack, "seq", axis=0, tiled=True),
        lax.all_gather(output_grad, "seq", axis=0, tiled=True),
        log_every,
        inner_every,
        key_heads,
        value_heads,
    )
    key_grad = join_heads((key_sum * HD ** (-0.5)).astype(jnp.bfloat16))
    value_grad = join_heads(value_sum.astype(jnp.bfloat16))
    back_first = (pick_entry(starts, peer_index) - device + devices - 1) // devices
    back_slot = back_first + within
    back_live = back_slot * devices + device < pick_entry(shard_ends, peer_index)
    back_row = jnp.clip(back_slot, 0, visible_rows - 1)

    def returning(block):
        return jnp.where(
            back_live[:, None], jnp.take(block, back_row, axis=0), jnp.zeros((), block.dtype)
        )

    returned = (
        lax.all_to_all(returning(query_grad), "seq", split_axis=0, concat_axis=0, tiled=True),
        lax.all_to_all(returning(key_grad), "seq", split_axis=0, concat_axis=0, tiled=True),
        lax.all_to_all(returning(value_grad), "seq", split_axis=0, concat_axis=0, tiled=True),
    )
    position = jnp.arange(frames, dtype=jnp.int32)
    visible = (position < span_begin) | (position >= span_begin + masked)
    frame_rank = jnp.where(position < span_begin, position, position - masked)
    frame_global = start_here + frame_rank
    frame_peer = frame_global % devices
    frame_slot = frame_global // devices
    frame_first = (start_here - frame_peer + devices - 1) // devices
    frame_row = jnp.clip(
        frame_peer * capacity + frame_slot - frame_first, 0, devices * capacity - 1
    )

    def placed(block):
        return jnp.where(
            visible[:, None], jnp.take(block, frame_row, axis=0), jnp.zeros((), block.dtype)
        )[None]

    return (placed(returned[0]), placed(returned[1]), placed(returned[2]), weight_grad)


def solution(mesh):
    placed = (
        P("clip", "seq", None),
        P("clip", "seq", None),
        P("clip", "seq", None),
        P("clip", "seq", None),
        P("clip", None),
        P("clip", None),
        P("seq", None),
    )
    return jax.shard_map(
        local,
        mesh=mesh,
        in_specs=placed,
        out_specs=(
            P("clip", "seq", None),
            P("clip", "seq", None),
            P("clip", "seq", None),
            P("seq", None),
        ),
        check_vma=False,
    )
```

profile of v0, /device:TPU:0, one launch (start us, length us, event | category | flops | bytes accessed | tf_op | source)
XLA Modules:
  0.0 217.8 jit_solution(15005196300830094414)
XLA Ops:
  7.2 1.0 reduce-window.4
  8.2 1.3 select_reduce_fusion.3
  11.5 1.3 broadcast_compare_fusion.1
  13.5 1.9 gather_fusion.2
  17.8 5.2 %all-to-all-start = ((bf16[8,12,512]{2,1,0:T(8,128)(2,1)}), bf16[8,12,512]{2,1,0:T(8,128)(2,1)S(1)}, u32[]{:S(2)}, u32[]{:S(2)}) async-start(bf16[8,12,512]{2,1,0:T(8,128)(2,1)} %all_to_all.54), calls=%async_computation | async-start | bytes 262144 | tf_op jit(solution)/shard_map/all_to_all | solution.py:124
  27.6 1.3 broadcast_compare_fusion
  29.8 4.2 %all-to-all-start.1 = ((bf16[8,12,512]{2,1,0:T(8,128)(2,1)}), bf16[8,12,512]{2,1,0:T(8,128)(2,1)S(1)}, u32[]{:S(2)}, u32[]{:S(2)}) async-start(bf16[8,12,512]{2,1,0:T(8,128)(2,1)} %all_to_all.57), calls=%async_computation.1 | async-start | bytes 262144 | tf_op jit(solution)/shard_map/all_to_all | solution.py:125
  34.0 6.9 %all-to-all-done.1 = bf16[8,12,512]{2,1,0:T(8,128)(2,1)S(1)} async-done(((bf16[8,12,512]{2,1,0:T(8,128)(2,1)}), bf16[8,12,512]{2,1,0:T(8,128)(2,1)S(1)}, u32[]{:S(2)}, u32[]{:S(2)}) %all-to-all-start.1) | async-done | bytes 98336 | tf_op jit(solution)/shard_map/all_to_all | solution.py:125
  40.9 3.4 %all-to-all-start.2 = ((bf16[8,12,512]{2,1,0:T(8,128)(2,1)}), bf16[8,12,512]{2,1,0:T(8,128)(2,1)S(1)}, u32[]{:S(2)}, u32[]{:S(2)}) async-start(bf16[8,12,512]{2,1,0:T(8,128)(2,1)} %all_to_all.60), calls=%async_computation.2 | async-start | bytes 262144 | tf_op jit(solution)/shard_map/all_to_all | solution.py:126
  46.3 4.7 %all-to-all-done.2 = bf16[8,12,512]{2,1,0:T(8,128)(2,1)S(1)} async-done(((bf16[8,12,512]{2,1,0:T(8,128)(2,1)}), bf16[8,12,512]{2,1,0:T(8,128)(2,1)S(1)}, u32[]{:S(2)}, u32[]{:S(2)}) %all-to-all-start.2) | async-done | bytes 98336 | tf_op jit(solution)/shard_map/all_to_all | solution.py:126
  51.1 3.4 %all-to-all-start.3 = ((bf16[8,12,1024]{2,1,0:T(8,128)(2,1)}), bf16[8,12,1024]{2,1,0:T(8,128)(2,1)S(1)}, u32[]{:S(2)}, u32[]{:S(2)}) async-start(bf16[8,12,1024]{2,1,0:T(8,128)(2,1)} %select_select_fusion.3), calls=%async_computation.3 | async-start | bytes 524288 | tf_op jit(solution)/shard_map/all_to_all | solution.py:127
  55.4 10.0 %all_gather.21 = bf16[384,512]{1,0:T(8,128)(2,1)S(1)} all-gather(bf16[48,512]{1,0:T(8,128)(2,1)S(1)} %get-tuple-element.249), channel_id=1, replica_groups=mesh['seq'=8,'clip'=4] {'seq'}, dimensions={0}, use_global_device_ids=true | all-gather | bytes 442368 | tf_op jit(solution)/shard_map/all_gather | solution.py:145
  65.7 9.5 %all_gather.22 = bf16[384,512]{1,0:T(8,128)(2,1)S(1)} all-gather(bf16[48,512]{1,0:T(8,128)(2,1)S(1)} %get-tuple-element.248), channel_id=1, replica_groups=mesh['seq'=8,'clip'=4] {'seq'}, dimensions={0}, use_global_device_ids=true | all-gather | bytes 442368 | tf_op jit(solution)/shard_map/all_gather | solution.py:146
  75.6 8.6 %all_gather.24 = bf16[384,512]{1,0:T(8,128)(2,1)S(1)} all-gather(bf16[48,512]{1,0:T(8,128)(2,1)S(1)} %get-tuple-element.250), channel_id=1, replica_groups=mesh['seq'=8,'clip'=4] {'seq'}, dimensions={0}, use_global_device_ids=true | all-gather | bytes 442368 | tf_op jit(solution)/shard_map/all_gather | solution.py:176
  85.3 1.7 convolution_convert_fusion.2
  87.1 9.5 %all_gather.26 = bf16[384,512]{1,0:T(8,128)(2,1)S(1)} all-gather(bf16[48,512]{1,0:T(8,128)(2,1)S(1)} %convolution_convert_fusion.2), channel_id=1, replica_groups=mesh['seq'=8,'clip'=4] {'seq'}, dimensions={0}, use_global_device_ids=true | all-gather | bytes 442368 | tf_op jit(solution)/shard_map/all_gather | solution.py:177
  96.6 18.4 %while.28 = (s32[]{:T(128)}, bf16[8,48,64]{2,1,0:T(8,128)(2,1)}, bf16[8,48,64]{2,1,0:T(8,128)(2,1)}, f32[8,48]{1,0:T(8,128)S(1)}, f32[8,48]{1,0:T(8,128)S(1)}, /...) while((s32[]{:T(128)}, bf16[8,48,64]{2,1,0:T(8,128)(2,1)}, ...), condition=%wide.region_12.15_spmd, body=%wide.region_8.14_spmd.sunk | while | flops 9642914 | bytes 566969 | solution.py:148
  97.1 0.8 bitcast_dynamic-update-slice_fusion.2
  98.0 0.9 fusion.124
  99.4 0.8 bitcast_dynamic-update-slice_fusion.2
  100.3 0.9 fusion.124
  101.7 0.8 bitcast_dynamic-update-slice_fusion.2
  102.6 0.9 fusion.124
  104.0 0.8 bitcast_dynamic-update-slice_fusion.2
  104.9 0.9 fusion.124
  106.3 0.8 bitcast_dynamic-update-slice_fusion.2
  107.2 0.9 fusion.124
  108.6 0.8 bitcast_dynamic-update-slice_fusion.2
  109.5 0.9 fusion.124
  110.9 0.8 bitcast_dynamic-update-slice_fusion.2
  111.8 0.9 fusion.124
  114.1 0.9 fusion.124
  115.1 8.3 %all-gather = f32[8,48,8]{1,2,0:T(8,128)S(1)} all-gather(f32[1,48,8]{1,2,0:T(8,128)S(1)} %bitcast.209), channel_id=1, replica_groups=mesh['seq'=8,'clip'=4] {'seq'}, dimensions={0}, use_global_device_ids=true | all-gather | bytes 13824 | tf_op jit(solution)/shard_map/all_gather | solution.py:170
  123.5 9.1 %all-gather.1 = f32[8,48,8]{1,2,0:T(8,128)S(1)} all-gather(f32[1,48,8]{1,2,0:T(8,128)S(1)} %bitcast.210), channel_id=1, replica_groups=mesh['seq'=8,'clip'=4] {'seq'}, dimensions={0}, use_global_device_ids=true | all-gather | bytes 13824 | tf_op jit(solution)/shard_map/all_gather | solution.py:171
  133.0 1.5 convolution_convert_fusion.1
  134.5 5.0 %while.29 = (s32[]{:T(128)}, f32[8,48,64]{2,1,0:T(8,128)S(1)}, bf16[8,48,64]{2,1,0:T(8,128)(2,1)S(1)}, bf16[8,384,64]{1,2,0:T(8,128)(2,1)S(1)}, bf16[8,48,64]{2,...) while((s32[]{:T(128)}, f32[8,48,64]{2,1,0:T(8,128)S(1)}, ...), condition=%wide.region_14.19_spmd, body=%wide.region_13.18_spmd.sunk | while | flops 9547778 | bytes 505961 | solution.py:80
  143.2 3.4 %all-to-all-start.4 = ((bf16[8,12,512]{2,1,0:T(8,128)(2,1)}), bf16[8,12,512]{2,1,0:T(8,128)(2,1)S(1)}, u32[]{:S(2)}, u32[]{:S(2)}) async-start(bf16[8,12,512]{2,1,0:T(8,128)(2,1)} %all_to_all.65), calls=%async_computation.4 | async-start | bytes 262144 | tf_op jit(solution)/shard_map/all_to_all | solution.py:196
  147.2 4.7 %all-to-all-done.4 = bf16[8,12,512]{2,1,0:T(8,128)(2,1)S(1)} async-done(((bf16[8,12,512]{2,1,0:T(8,128)(2,1)}), bf16[8,12,512]{2,1,0:T(8,128)(2,1)S(1)}, u32[]{:S(2)}, u32[]{:S(2)}) %all-to-all-start.4) | async-done | bytes 98336 | tf_op jit(solution)/shard_map/all_to_all | solution.py:196
  152.0 3.4 %all-to-all-start.5 = ((bf16[8,12,512]{2,1,0:T(8,128)(2,1)}), bf16[8,12,512]{2,1,0:T(8,128)(2,1)S(1)}, u32[]{:S(2)}, u32[]{:S(2)}) async-start(bf16[8,12,512]{2,1,0:T(8,128)(2,1)} %all_to_all.68), calls=%async_computation.5 | async-start | bytes 262144 | tf_op jit(solution)/shard_map/all_to_all | solution.py:197
  156.7 5.5 %all-to-all-done.5 = bf16[8,12,512]{2,1,0:T(8,128)(2,1)S(1)} async-done(((bf16[8,12,512]{2,1,0:T(8,128)(2,1)}), bf16[8,12,512]{2,1,0:T(8,128)(2,1)S(1)}, u32[]{:S(2)}, u32[]{:S(2)}) %all-to-all-start.5) | async-done | bytes 98336 | tf_op jit(solution)/shard_map/all_to_all | solution.py:197
  162.2 3.4 %all-to-all-start.6 = ((bf16[8,12,512]{2,1,0:T(8,128)(2,1)}), bf16[8,12,512]{2,1,0:T(8,128)(2,1)S(1)}, u32[]{:S(2)}, u32[]{:S(2)}) async-start(bf16[8,12,512]{2,1,0:T(8,128)(2,1)} %all_to_all.71), calls=%async_computation.6 | async-start | bytes 262144 | tf_op jit(solution)/shard_map/all_to_all | solution.py:198
  165.9 2.0 gather_fusion.9
  167.9 2.0 gather_fusion.11
  169.9 1.7 all-to-all-done.6
  171.7 2.0 gather_fusion.13
  173.7 1.4 fusion.64
  175.1 34.6 %all-reduce.2.cloned.1.call-done = bf16[64,1024]{1,0:T(8,128)(2,1)} async-done(((bf16[64,1024]{1,0:T(8,128)(2,1)}), bf16[64,1024]{1,0:T(8,128)(2,1)}) %all-reduce.2.cloned.1.call-update) | async-done | bytes 131088 | tf_op jit(solution)/shard_map/psum | solution.py:167
  209.7 1.6 convert_multiply_fusion
  (183 shorter events, 30.0 us)
Async XLA Ops:
  7.2 19.5 %copy-start = (bf16[1,512,1024]{2,1,0:T(8,128)(2,1)S(1)}, bf16[1,512,1024]{2,1,0:T(8,128)(2,1)}, u32[]{:S(2)}) copy-start(bf16[1,512,1024]{2,1,0:T(8,128)(2,1)} %param.22) | copy-start | bytes 3145732
  7.2 8.2 %copy-start.1 = (bf16[1,512,512]{2,1,0:T(8,128)(2,1)S(1)}, bf16[1,512,512]{2,1,0:T(8,128)(2,1)}, u32[]{:S(2)}) copy-start(bf16[1,512,512]{2,1,0:T(8,128)(2,1)} %param.20) | copy-start | bytes 1572868
  7.2 9.0 %copy-start.2 = (bf16[1,512,512]{2,1,0:T(8,128)(2,1)S(1)}, bf16[1,512,512]{2,1,0:T(8,128)(2,1)}, u32[]{:S(2)}) copy-start(bf16[1,512,512]{2,1,0:T(8,128)(2,1)} %param.21) | copy-start | bytes 1572868
  17.8 12.0 %all-to-all-start = ((bf16[8,12,512]{2,1,0:T(8,128)(2,1)}), bf16[8,12,512]{2,1,0:T(8,128)(2,1)S(1)}, u32[]{:S(2)}, u32[]{:S(2)}) async-start(bf16[8,12,512]{2,1,0:T(8,128)(2,1)} %all_to_all.54), calls=%async_computation | async-start | bytes 262144 | tf_op jit(solution)/shard_map/all_to_all | solution.py:124
  23.0 62.3 %all-gather.4.cloned.1.call-start = ((), (), s32[]{:S(2)}) async-start(), calls=%async_computation.8 | async-start | bytes 1179648 | tf_op jit(solution)/shard_map/all_gather | solution.py:140
  29.8 11.1 %all-to-all-start.1 = ((bf16[8,12,512]{2,1,0:T(8,128)(2,1)}), bf16[8,12,512]{2,1,0:T(8,128)(2,1)S(1)}, u32[]{:S(2)}, u32[]{:S(2)}) async-start(bf16[8,12,512]{2,1,0:T(8,128)(2,1)} %all_to_all.57), calls=%async_computation.1 | async-start | bytes 262144 | tf_op jit(solution)/shard_map/all_to_all | solution.py:125
  40.9 10.2 %all-to-all-start.2 = ((bf16[8,12,512]{2,1,0:T(8,128)(2,1)}), bf16[8,12,512]{2,1,0:T(8,128)(2,1)S(1)}, u32[]{:S(2)}, u32[]{:S(2)}) async-start(bf16[8,12,512]{2,1,0:T(8,128)(2,1)} %all_to_all.60), calls=%async_computation.2 | async-start | bytes 262144 | tf_op jit(solution)/shard_map/all_to_all | solution.py:126
  51.1 33.5 %all-to-all-start.3 = ((bf16[8,12,1024]{2,1,0:T(8,128)(2,1)}), bf16[8,12,1024]{2,1,0:T(8,128)(2,1)S(1)}, u32[]{:S(2)}, u32[]{:S(2)}) async-start(bf16[8,12,1024]{2,1,0:T(8,128)(2,1)} %select_select_fusion.3), calls=%async_computation.3 | async-start | bytes 524288 | tf_op jit(solution)/shard_map/all_to_all | solution.py:127
  54.5 119.2 %reduce-scatter.2.cloned.1.call-start = ((), (), s32[]{:S(2)}) async-start(), calls=%async_computation.9 | async-start | bytes 1179648 | tf_op jit(solution)/shard_map/reduce_scatter | solution.py:164
  115.1 17.8 %copy-start.4 = (bf16[8,48,64]{2,1,0:T(8,128)(2,1)S(1)}, bf16[8,48,64]{2,1,0:T(8,128)(2,1)}, u32[]{:S(2)}) copy-start(bf16[8,48,64]{2,1,0:T(8,128)(2,1)} %get-tuple-element.111) | copy-start | bytes 147460
  133.0 1.5 copy-start.3
  139.7 1.7 copy-start.5
  143.2 8.8 %all-to-all-start.4 = ((bf16[8,12,512]{2,1,0:T(8,128)(2,1)}), bf16[8,12,512]{2,1,0:T(8,128)(2,1)S(1)}, u32[]{:S(2)}, u32[]{:S(2)}) async-start(bf16[8,12,512]{2,1,0:T(8,128)(2,1)} %all_to_all.65), calls=%async_computation.4 | async-start | bytes 262144 | tf_op jit(solution)/shard_map/all_to_all | solution.py:196
  152.0 10.3 %all-to-all-start.5 = ((bf16[8,12,512]{2,1,0:T(8,128)(2,1)}), bf16[8,12,512]{2,1,0:T(8,128)(2,1)S(1)}, u32[]{:S(2)}, u32[]{:S(2)}) async-start(bf16[8,12,512]{2,1,0:T(8,128)(2,1)} %all_to_all.68), calls=%async_computation.5 | async-start | bytes 262144 | tf_op jit(solution)/shard_map/all_to_all | solution.py:197
  162.2 9.4 %all-to-all-start.6 = ((bf16[8,12,512]{2,1,0:T(8,128)(2,1)}), bf16[8,12,512]{2,1,0:T(8,128)(2,1)S(1)}, u32[]{:S(2)}, u32[]{:S(2)}) async-start(bf16[8,12,512]{2,1,0:T(8,128)(2,1)} %all_to_all.71), calls=%async_computation.6 | async-start | bytes 262144 | tf_op jit(solution)/shard_map/all_to_all | solution.py:198
  165.6 44.0 %all-reduce.2.cloned.1.call-start = ((), (), s32[]{:S(2)}) async-start(), calls=%async_computation.10 | async-start | bytes 262144 | tf_op jit(solution)/shard_map/psum | solution.py:167
Sparse Core Ops, SparseCore 0:
  25.7 27.5 all-gather.3
  134.6 38.3 reduce-scatter.1
  175.3 34.3 all-reduce.1
where the time goes:
time: 219 us; the launch traced here: 218 us
  waiting for transfers between devices  59 us (27%)
  blocking collectives  55 us (25%)
  starting transfers between devices  26.6 us (12%)
  matrix products  23 us (11%)
  local copies, waits for them, and re-layouts  22.3 us (10%)
  between operations  16.3 us (7%)
  other arithmetic  15.3 us (7%)
    psum x1, waiting for transfers between devices, local(): clip_sum = lax.psum(seq_sum, 'clip').astype(jnp.float32)  34.6 us
    all_gather x1, blocking collectives, local(): lax.all_gather(key_pack, 'seq', axis=0, tiled=True)  9.95 us
    all_gather x1, blocking collectives, local(): lax.all_gather(value_pack, 'seq', axis=0, tiled=True)  9.54 us
    all_gather x1, blocking collectives, local(): lax.all_gather(output_grad, 'seq', axis=0, tiled=True)  9.54 us
    all_gather x1, blocking collectives, local(): lax.all_gather(inner_rows, 'seq', axis=0, tiled=True)  9.06 us
    all_gather x1, blocking collectives, local(): lax.all_gather(query_pack, 'seq', axis=0, tiled=True)  8.62 us
    all_gather x1, blocking collectives, local(): lax.all_gather(log_rows, 'seq', axis=0, tiled=True)  8.29 us
    dot_general x8, matrix products, query_side(): jnp.dot(dscores, key_head, preferred_element_type=jnp.float32) * factor  6.93 us
  transfers between devices with their start and end apart: 10, of which 6 were waited for; matrix products, arithmetic and copies ran while one was open for 11% of the time, Pallas kernels for 0%

commit v1 on v0

--- a/solution.py
+++ b/solution.py
@@ -164,7 +164,7 @@
     seq_sum = lax.psum_scatter(
         partial_term.astype(jnp.bfloat16), "seq", scatter_dimension=0, tiled=True
     )
-    clip_sum = lax.psum(seq_sum, "clip").astype(jnp.float32)
+    clip_sum = jnp.sum(lax.all_gather(seq_sum, "clip"), axis=0).astype(jnp.float32)
     weight_grad = clip_sum * (lax.axis_size("clip") * visible_rows * devices) ** (-0.5)
     log_every, inner_every = (
         lax.all_gather(log_rows, "seq", axis=0, tiled=True),

time: 219 us -> 199 us (0.909)
  waiting for transfers between devices: 59 us -> 24.4 us
  blocking collectives: 55 us -> 70.1 us
    psum x1 -> x0, waiting for transfers between devices: 34.6 us -> none  [local(): clip_sum = lax.psum(seq_sum, 'clip').astype(jnp.float32)]
    all_gather x0 -> x1, blocking collectives: none -> 15.1 us  [local(): lax.all_gather(seq_sum, 'clip')]
  transfers between devices with their start and end apart: 10 -> 9, of which waited for: 6 -> 5; matrix products, arithmetic and copies ran while one was open for 11% -> 12% of each run, Pallas kernels for 0% -> 0%
where the time goes in v1:
time: 199 us; the launch traced here: 198 us
  blocking collectives  70.1 us (35%)
  starting transfers between devices  26.6 us (13%)
  waiting for transfers between devices  24.4 us (12%)
  matrix products  23 us (12%)
  local copies, waits for them, and re-layouts  22.3 us (11%)
  between operations  16.5 us (8%)
  other arithmetic  14.5 us (7%)
    all_gather x1, blocking collectives, local(): lax.all_gather(seq_sum, 'clip')  15.1 us
    all_gather x1, blocking collectives, local(): lax.all_gather(key_pack, 'seq', axis=0, tiled=True)  9.95 us
    all_gather x1, blocking collectives, local(): lax.all_gather(value_pack, 'seq', axis=0, tiled=True)  9.54 us
    all_gather x1, blocking collectives, local(): lax.all_gather(output_grad, 'seq', axis=0, tiled=True)  9.54 us
    all_gather x1, blocking collectives, local(): lax.all_gather(inner_rows, 'seq', axis=0, tiled=True)  9.06 us
    all_gather x1, blocking collectives, local(): lax.all_gather(query_pack, 'seq', axis=0, tiled=True)  8.62 us
    all_gather x1, blocking collectives, local(): lax.all_gather(log_rows, 'seq', axis=0, tiled=True)  8.29 us
    dot_general x8, matrix products, query_side(): jnp.dot(dscores, key_head, preferred_element_type=jnp.float32) * factor  6.93 us
  transfers between devices with their start and end apart: 9, of which 5 were waited for; matrix products, arithmetic and copies ran while one was open for 12% of the time, Pallas kernels for 0%

profile of v1, /device:TPU:0, one launch (start us, length us, event | category | flops | bytes accessed | tf_op | source)
XLA Modules:
  0.0 197.8 jit_solution(14398295590541453359)
XLA Ops:
  7.2 1.0 reduce-window.4
  8.2 1.3 select_reduce_fusion.3
  11.5 1.3 broadcast_compare_fusion.1
  13.5 1.9 gather_fusion.2
  17.8 5.2 %all-to-all-start = ((bf16[8,12,512]{2,1,0:T(8,128)(2,1)}), bf16[8,12,512]{2,1,0:T(8,128)(2,1)S(1)}, u32[]{:S(2)}, u32[]{:S(2)}) async-start(bf16[8,12,512]{2,1,0:T(8,128)(2,1)} %all_to_all.54), calls=%async_computation | async-start | bytes 262144 | tf_op jit(solution)/shard_map/all_to_all | solution.py:124
  27.6 1.3 broadcast_compare_fusion
  29.0 0.8 select_select_fusion.3
  29.8 4.2 %all-to-all-start.1 = ((bf16[8,12,512]{2,1,0:T(8,128)(2,1)}), bf16[8,12,512]{2,1,0:T(8,128)(2,1)S(1)}, u32[]{:S(2)}, u32[]{:S(2)}) async-start(bf16[8,12,512]{2,1,0:T(8,128)(2,1)} %all_to_all.57), calls=%async_computation.1 | async-start | bytes 262144 | tf_op jit(solution)/shard_map/all_to_all | solution.py:125
  34.0 6.9 %all-to-all-done.1 = bf16[8,12,512]{2,1,0:T(8,128)(2,1)S(1)} async-done(((bf16[8,12,512]{2,1,0:T(8,128)(2,1)}), bf16[8,12,512]{2,1,0:T(8,128)(2,1)S(1)}, u32[]{:S(2)}, u32[]{:S(2)}) %all-to-all-start.1) | async-done | bytes 98336 | tf_op jit(solution)/shard_map/all_to_all | solution.py:125
  40.9 3.4 %all-to-all-start.2 = ((bf16[8,12,512]{2,1,0:T(8,128)(2,1)}), bf16[8,12,512]{2,1,0:T(8,128)(2,1)S(1)}, u32[]{:S(2)}, u32[]{:S(2)}) async-start(bf16[8,12,512]{2,1,0:T(8,128)(2,1)} %all_to_all.60), calls=%async_computation.2 | async-start | bytes 262144 | tf_op jit(solution)/shard_map/all_to_all | solution.py:126
  46.3 4.7 %all-to-all-done.2 = bf16[8,12,512]{2,1,0:T(8,128)(2,1)S(1)} async-done(((bf16[8,12,512]{2,1,0:T(8,128)(2,1)}), bf16[8,12,512]{2,1,0:T(8,128)(2,1)S(1)}, u32[]{:S(2)}, u32[]{:S(2)}) %all-to-all-start.2) | async-done | bytes 98336 | tf_op jit(solution)/shard_map/all_to_all | solution.py:126
  51.1 3.4 %all-to-all-start.3 = ((bf16[8,12,1024]{2,1,0:T(8,128)(2,1)}), bf16[8,12,1024]{2,1,0:T(8,128)(2,1)S(1)}, u32[]{:S(2)}, u32[]{:S(2)}) async-start(bf16[8,12,1024]{2,1,0:T(8,128)(2,1)} %select_select_fusion.3), calls=%async_computation.3 | async-start | bytes 524288 | tf_op jit(solution)/shard_map/all_to_all | solution.py:127
  55.4 10.0 %all_gather.27 = bf16[384,512]{1,0:T(8,128)(2,1)S(1)} all-gather(bf16[48,512]{1,0:T(8,128)(2,1)S(1)} %get-tuple-element.249), channel_id=1, replica_groups=mesh['seq'=8,'clip'=4] {'seq'}, dimensions={0}, use_global_device_ids=true | all-gather | bytes 442368 | tf_op jit(solution)/shard_map/all_gather | solution.py:145
  65.7 9.5 %all_gather.28 = bf16[384,512]{1,0:T(8,128)(2,1)S(1)} all-gather(bf16[48,512]{1,0:T(8,128)(2,1)S(1)} %get-tuple-element.248), channel_id=1, replica_groups=mesh['seq'=8,'clip'=4] {'seq'}, dimensions={0}, use_global_device_ids=true | all-gather | bytes 442368 | tf_op jit(solution)/shard_map/all_gather | solution.py:146
  75.6 8.6 %all_gather.30 = bf16[384,512]{1,0:T(8,128)(2,1)S(1)} all-gather(bf16[48,512]{1,0:T(8,128)(2,1)S(1)} %get-tuple-element.250), channel_id=1, replica_groups=mesh['seq'=8,'clip'=4] {'seq'}, dimensions={0}, use_global_device_ids=true | all-gather | bytes 442368 | tf_op jit(solution)/shard_map/all_gather | solution.py:176
  85.3 1.7 convolution_convert_fusion.2
  87.1 9.5 %all_gather.32 = bf16[384,512]{1,0:T(8,128)(2,1)S(1)} all-gather(bf16[48,512]{1,0:T(8,128)(2,1)S(1)} %convolution_convert_fusion.2), channel_id=1, replica_groups=mesh['seq'=8,'clip'=4] {'seq'}, dimensions={0}, use_global_device_ids=true | all-gather | bytes 442368 | tf_op jit(solution)/shard_map/all_gather | solution.py:177
  96.6 18.4 %while.28 = (s32[]{:T(128)}, bf16[8,48,64]{2,1,0:T(8,128)(2,1)}, bf16[8,48,64]{2,1,0:T(8,128)(2,1)}, f32[8,48]{1,0:T(8,128)S(1)}, f32[8,48]{1,0:T(8,128)S(1)}, /...) while((s32[]{:T(128)}, bf16[8,48,64]{2,1,0:T(8,128)(2,1)}, ...), condition=%wide.region_12.15_spmd, body=%wide.region_8.14_spmd.sunk | while | flops 9642914 | bytes 566969 | solution.py:148
  97.1 0.8 bitcast_dynamic-update-slice_fusion.2
  98.0 0.9 fusion.124
  99.4 0.8 bitcast_dynamic-update-slice_fusion.2
  100.3 0.9 fusion.124
  101.7 0.8 bitcast_dynamic-update-slice_fusion.2
  102.6 0.9 fusion.124
  104.0 0.8 bitcast_dynamic-update-slice_fusion.2
  104.9 0.9 fusion.124
  106.3 0.8 bitcast_dynamic-update-slice_fusion.2
  107.2 0.9 fusion.124
  108.6 0.8 bitcast_dynamic-update-slice_fusion.2
  109.5 0.9 fusion.124
  110.9 0.8 bitcast_dynamic-update-slice_fusion.2
  111.8 0.9 fusion.124
  114.1 0.9 fusion.124
  115.1 8.3 %all-gather.1 = f32[8,48,8]{1,2,0:T(8,128)S(1)} all-gather(f32[1,48,8]{1,2,0:T(8,128)S(1)} %bitcast.211), channel_id=1, replica_groups=mesh['seq'=8,'clip'=4] {'seq'}, dimensions={0}, use_global_device_ids=true | all-gather | bytes 13824 | tf_op jit(solution)/shard_map/all_gather | solution.py:170
  123.5 9.1 %all-gather.2 = f32[8,48,8]{1,2,0:T(8,128)S(1)} all-gather(f32[1,48,8]{1,2,0:T(8,128)S(1)} %bitcast.212), channel_id=1, replica_groups=mesh['seq'=8,'clip'=4] {'seq'}, dimensions={0}, use_global_device_ids=true | all-gather | bytes 13824 | tf_op jit(solution)/shard_map/all_gather | solution.py:171
  133.0 1.5 convolution_convert_fusion.1
  134.5 5.0 %while.29 = (s32[]{:T(128)}, f32[8,48,64]{2,1,0:T(8,128)S(1)}, bf16[8,48,64]{2,1,0:T(8,128)(2,1)S(1)}, bf16[8,384,64]{1,2,0:T(8,128)(2,1)S(1)}, bf16[8,48,64]{2,...) while((s32[]{:T(128)}, f32[8,48,64]{2,1,0:T(8,128)S(1)}, ...), condition=%wide.region_14.19_spmd, body=%wide.region_13.18_spmd.sunk | while | flops 9547778 | bytes 505961 | solution.py:80
  143.2 3.4 %all-to-all-start.4 = ((bf16[8,12,512]{2,1,0:T(8,128)(2,1)}), bf16[8,12,512]{2,1,0:T(8,128)(2,1)S(1)}, u32[]{:S(2)}, u32[]{:S(2)}) async-start(bf16[8,12,512]{2,1,0:T(8,128)(2,1)} %all_to_all.65), calls=%async_computation.4 | async-start | bytes 262144 | tf_op jit(solution)/shard_map/all_to_all | solution.py:196
  147.2 4.7 %all-to-all-done.4 = bf16[8,12,512]{2,1,0:T(8,128)(2,1)S(1)} async-done(((bf16[8,12,512]{2,1,0:T(8,128)(2,1)}), bf16[8,12,512]{2,1,0:T(8,128)(2,1)S(1)}, u32[]{:S(2)}, u32[]{:S(2)}) %all-to-all-start.4) | async-done | bytes 98336 | tf_op jit(solution)/shard_map/all_to_all | solution.py:196
  152.0 3.4 %all-to-all-start.5 = ((bf16[8,12,512]{2,1,0:T(8,128)(2,1)}), bf16[8,12,512]{2,1,0:T(8,128)(2,1)S(1)}, u32[]{:S(2)}, u32[]{:S(2)}) async-start(bf16[8,12,512]{2,1,0:T(8,128)(2,1)} %all_to_all.68), calls=%async_computation.5 | async-start | bytes 262144 | tf_op jit(solution)/shard_map/all_to_all | solution.py:197
  156.7 5.5 %all-to-all-done.5 = bf16[8,12,512]{2,1,0:T(8,128)(2,1)S(1)} async-done(((bf16[8,12,512]{2,1,0:T(8,128)(2,1)}), bf16[8,12,512]{2,1,0:T(8,128)(2,1)S(1)}, u32[]{:S(2)}, u32[]{:S(2)}) %all-to-all-start.5) | async-done | bytes 98336 | tf_op jit(solution)/shard_map/all_to_all | solution.py:197
  162.2 3.6 %all-to-all-start.6 = ((bf16[8,12,512]{2,1,0:T(8,128)(2,1)}), bf16[8,12,512]{2,1,0:T(8,128)(2,1)S(1)}, u32[]{:S(2)}, u32[]{:S(2)}) async-start(bf16[8,12,512]{2,1,0:T(8,128)(2,1)} %all_to_all.71), calls=%async_computation.6 | async-start | bytes 262144 | tf_op jit(solution)/shard_map/all_to_all | solution.py:198
  165.9 2.0 gather_fusion.9
  167.9 2.0 gather_fusion.11
  169.9 1.8 all-to-all-done.6
  171.7 2.0 gather_fusion.13
  173.7 1.4 fusion.64
  175.1 15.1 %all-gather = bf16[256,1024]{1,0:T(8,128)(2,1)S(1)} all-gather(bf16[64,1024]{1,0:T(8,128)(2,1)} %reduce-scatter.2.cloned.1.call-done), channel_id=2, replica_groups=mesh['seq'=8,'clip'=4] {'clip'}, dimensions={0}, use_global_device_ids=true | all-gather | bytes 655360 | tf_op jit(solution)/shard_map/all_gather | solution.py:167
  (182 shorter events, 29.8 us)
Async XLA Ops:
  7.2 19.5 %copy-start = (bf16[1,512,1024]{2,1,0:T(8,128)(2,1)S(1)}, bf16[1,512,1024]{2,1,0:T(8,128)(2,1)}, u32[]{:S(2)}) copy-start(bf16[1,512,1024]{2,1,0:T(8,128)(2,1)} %param.22) | copy-start | bytes 3145732
  7.2 8.2 %copy-start.1 = (bf16[1,512,512]{2,1,0:T(8,128)(2,1)S(1)}, bf16[1,512,512]{2,1,0:T(8,128)(2,1)}, u32[]{:S(2)}) copy-start(bf16[1,512,512]{2,1,0:T(8,128)(2,1)} %param.20) | copy-start | bytes 1572868
  7.2 9.0 %copy-start.2 = (bf16[1,512,512]{2,1,0:T(8,128)(2,1)S(1)}, bf16[1,512,512]{2,1,0:T(8,128)(2,1)}, u32[]{:S(2)}) copy-start(bf16[1,512,512]{2,1,0:T(8,128)(2,1)} %param.21) | copy-start | bytes 1572868
  17.8 12.0 %all-to-all-start = ((bf16[8,12,512]{2,1,0:T(8,128)(2,1)}), bf16[8,12,512]{2,1,0:T(8,128)(2,1)S(1)}, u32[]{:S(2)}, u32[]{:S(2)}) async-start(bf16[8,12,512]{2,1,0:T(8,128)(2,1)} %all_to_all.54), calls=%async_computation | async-start | bytes 262144 | tf_op jit(solution)/shard_map/all_to_all | solution.py:124
  23.0 62.3 %all-gather.5.cloned.1.call-start = ((), (), s32[]{:S(2)}) async-start(), calls=%async_computation.8 | async-start | bytes 1179648 | tf_op jit(solution)/shard_map/all_gather | solution.py:140
  29.8 11.1 %all-to-all-start.1 = ((bf16[8,12,512]{2,1,0:T(8,128)(2,1)}), bf16[8,12,512]{2,1,0:T(8,128)(2,1)S(1)}, u32[]{:S(2)}, u32[]{:S(2)}) async-start(bf16[8,12,512]{2,1,0:T(8,128)(2,1)} %all_to_all.57), calls=%async_computation.1 | async-start | bytes 262144 | tf_op jit(solution)/shard_map/all_to_all | solution.py:125
  40.9 10.2 %all-to-all-start.2 = ((bf16[8,12,512]{2,1,0:T(8,128)(2,1)}), bf16[8,12,512]{2,1,0:T(8,128)(2,1)S(1)}, u32[]{:S(2)}, u32[]{:S(2)}) async-start(bf16[8,12,512]{2,1,0:T(8,128)(2,1)} %all_to_all.60), calls=%async_computation.2 | async-start | bytes 262144 | tf_op jit(solution)/shard_map/all_to_all | solution.py:126
  51.1 33.5 %all-to-all-start.3 = ((bf16[8,12,1024]{2,1,0:T(8,128)(2,1)}), bf16[8,12,1024]{2,1,0:T(8,128)(2,1)S(1)}, u32[]{:S(2)}, u32[]{:S(2)}) async-start(bf16[8,12,1024]{2,1,0:T(8,128)(2,1)} %select_select_fusion.3), calls=%async_computation.3 | async-start | bytes 524288 | tf_op jit(solution)/shard_map/all_to_all | solution.py:127
  54.5 120.6 %reduce-scatter.2.cloned.1.call-start = ((), (), s32[]{:S(2)}) async-start(), calls=%async_computation.9 | async-start | bytes 1179648 | tf_op jit(solution)/shard_map/reduce_scatter | solution.py:164
  115.1 17.8 %copy-start.4 = (bf16[8,48,64]{2,1,0:T(8,128)(2,1)S(1)}, bf16[8,48,64]{2,1,0:T(8,128)(2,1)}, u32[]{:S(2)}) copy-start(bf16[8,48,64]{2,1,0:T(8,128)(2,1)} %get-tuple-element.111) | copy-start | bytes 147460
  133.0 1.5 copy-start.3
  139.7 1.7 copy-start.5
  143.2 8.8 %all-to-all-start.4 = ((bf16[8,12,512]{2,1,0:T(8,128)(2,1)}), bf16[8,12,512]{2,1,0:T(8,128)(2,1)S(1)}, u32[]{:S(2)}, u32[]{:S(2)}) async-start(bf16[8,12,512]{2,1,0:T(8,128)(2,1)} %all_to_all.65), calls=%async_computation.4 | async-start | bytes 262144 | tf_op jit(solution)/shard_map/all_to_all | solution.py:196
  152.0 10.3 %all-to-all-start.5 = ((bf16[8,12,512]{2,1,0:T(8,128)(2,1)}), bf16[8,12,512]{2,1,0:T(8,128)(2,1)S(1)}, u32[]{:S(2)}, u32[]{:S(2)}) async-start(bf16[8,12,512]{2,1,0:T(8,128)(2,1)} %all_to_all.68), calls=%async_computation.5 | async-start | bytes 262144 | tf_op jit(solution)/shard_map/all_to_all | solution.py:197
  162.2 9.4 %all-to-all-start.6 = ((bf16[8,12,512]{2,1,0:T(8,128)(2,1)}), bf16[8,12,512]{2,1,0:T(8,128)(2,1)S(1)}, u32[]{:S(2)}, u32[]{:S(2)}) async-start(bf16[8,12,512]{2,1,0:T(8,128)(2,1)} %all_to_all.71), calls=%async_computation.6 | async-start | bytes 262144 | tf_op jit(solution)/shard_map/all_to_all | solution.py:198
Sparse Core Ops, SparseCore 0:
  25.7 27.5 all-gather.4
  134.6 38.3 reduce-scatter.1
